TPU v7x, 512 devices: a whole 4x4x16 slice. The times are simulated.
512 devices in a mesh: grp: 16 (over z), dev: 32 (over x, y, core).
Axes of the slice: x: 4, y: 4, z: 16, core: 2. Of those that a mesh axis runs over, the one named last changes fastest.
Arguments:
- stiff_rows: bfloat16 [512, 6, 384, 384], P(('grp', 'dev')), may hold values from -0.75 to 0.75
- stiff_iface: bfloat16 [512, 2, 384, 384], P(('grp', 'dev')), may hold values from -0.75 to 0.75
- columns: int32 [512, 6], P(('grp', 'dev')), may hold values from 0 to 31, as said below
- live_count: int32 [512], P(('grp', 'dev')), may hold values from 2 to 6
- aggregate: int32 [512], P(('grp', 'dev')), may hold values from 0 to 1
- prolong: bfloat16 [512, 384, 384], P(('grp', 'dev')), may hold values from -0.3125 to 0.3125
Outputs:
- coarse_band: float32 [12288, 2304], P(('grp', 'dev'))
Inputs may be any that keep to these rules, and one draw needn't show every extreme that they name: The 6 columns of a row are distinct, the first is the row's own position p, and each lies within 3 positions of p around the cycle of 32 positions of the slab.
All inputs are finite; a program needn't handle non-finite values.
Results may differ from a plain program's by a relative error of at most 0.018.
Values may be sent and summed in bfloat16 or wider, within the bound.
A program may use at most 64 MiB of HBM per device.

v0:
```python
import jax
import jax.numpy as jnp
from jax import lax
from jax.sharding import PartitionSpec as P

NB = 384
SLOTS = 6
REACH = 3
COARSE = 2


def passed_along(block, axis, distance):
    devices = range(lax.axis_size(axis))
    route = [((i - distance) % len(devices), i) for i in devices]
    return lax.ppermute(block, axis, route)


def extended(array, sides, width):
    for axis, dim in sides:
        count, length = (lax.axis_size(axis), array.shape[dim])
        up = [(i, (i + 1) % count) for i in range(count - 1)]
        down = [(j, i) for i, j in up]
        last = lax.slice_in_dim(array, length - width, length, axis=dim)
        initial = lax.slice_in_dim(array, 0, width, axis=dim)
        before = lax.ppermute(last, axis, up)
        after = lax.ppermute(initial, axis, down)
        array = jnp.concatenate([before, array, after], axis=dim)
    return array


def on_device(stiff_rows, stiff_iface, columns, live_count, aggregate, prolong):
    dev_count = lax.axis_size("dev")
    grp_count = lax.axis_size("grp")
    group_at = lax.axis_index("grp")
    place_at = lax.axis_index("dev")
    my_columns = columns[0]
    block_list = []
    agg_list = []
    for offset in range(-REACH, REACH + 1):
        if offset == 0:
            block_list.append(prolong)
            agg_list.append(aggregate)
        else:
            got = passed_along((prolong, aggregate), "dev", -offset)
            block_list.append(got[0])
            agg_list.append(got[1])
    window_blocks = jnp.concatenate(block_list, axis=0)
    window_aggs = jnp.concatenate(agg_list, axis=0)
    offsets = (my_columns - place_at + dev_count + REACH) % dev_count
    panels = jnp.take(window_blocks, offsets, axis=0)
    column_aggs = jnp.take(window_aggs, offsets, axis=0)
    slab_blocks, slab_aggs = (
        extended(prolong, (("grp", 0),), 1),
        extended(aggregate, (("grp", 0),), 1),
    )
    blocks = jnp.concatenate([panels, slab_blocks[0:1], slab_blocks[2:3]], axis=0)
    stiff = jnp.concatenate([stiff_rows[0], stiff_iface[0]], axis=0)
    qmat = jnp.einsum("kfg,kgm->kfm", stiff, blocks, preferred_element_type=jnp.float32).astype(
        jnp.bfloat16
    )
    contrib = jnp.einsum("fc,kfm->kcm", prolong[0], qmat, preferred_element_type=jnp.float32)
    low_agg = slab_aggs[0]
    up_agg = slab_aggs[2]
    targets = jnp.concatenate([column_aggs, low_agg[None], up_agg[None]])
    weights = jnp.concatenate(
        [
            (jnp.arange(SLOTS, dtype=jnp.int32) < live_count[0]).astype(jnp.float32),
            (group_at > 0).astype(jnp.float32)[None],
            (group_at < grp_count - 1).astype(jnp.float32)[None],
        ]
    )
    sides = jnp.concatenate([jnp.ones((SLOTS,), jnp.int32), jnp.array([0, 2], jnp.int32)])
    side_hot = (sides[:, None] == jnp.arange(3, dtype=jnp.int32)[None, :]).astype(jnp.float32)
    block_hot = (targets[:, None] == jnp.arange(COARSE, dtype=jnp.int32)[None, :]).astype(
        jnp.float32
    )
    placing = side_hot[:, :, None] * block_hot[:, None, :] * weights[:, None, None]
    partial_value = jnp.einsum("ksb,kcm->csbm", placing, contrib).reshape(NB, 3 * COARSE * NB)
    partial_value = partial_value.astype(jnp.bfloat16).astype(jnp.float32)
    own_hot = (jnp.arange(COARSE, dtype=jnp.int32) == aggregate[0]).astype(jnp.float32)
    spread = (own_hot[:, None, None] * partial_value[None]).reshape(COARSE * NB, 3 * COARSE * NB)
    return lax.psum_scatter(
        spread.astype(jnp.bfloat16), "dev", scatter_dimension=0, tiled=True
    ).astype(jnp.float32)


def solution(mesh):
    in_specs = (
        P(("grp", "dev"), None, None, None),
        P(("grp", "dev"), None, None, None),
        P(("grp", "dev"), None),
        P(("grp", "dev")),
        P(("grp", "dev")),
        P(("grp", "dev"), None, None),
    )
    out_specs = P(("grp", "dev"), None)
    return jax.shard_map(
        on_device, mesh=mesh, in_specs=in_specs, out_specs=out_specs, check_vma=False
    )
```

profile of v0, /device:TPU:1, one launch (start us, length us, event | category | flops | bytes accessed | tf_op | source)
XLA Modules:
  0.0 217.1 jit_solution(7227176308852019016)
XLA Ops:
  6.5 0.0 copy-start
  6.5 0.0 reduce-scatter.2.cloned.1.call-start
  6.5 4.7 %collective-permute-start.10 = (s32[1]{0:T(128)}, s32[1]{0:T(128)}, u32[]{:S(2)}, u32[]{:S(2)}) collective-permute-start(s32[1]{0:T(128)} %param.11), channel_id=1, source_target_pairs={{31,0},{0,1},{1,2},{2,3},{3,4},{4,5},{5,6},{6,7},{7,8},{8,9},{9,10... | collective-permute-start | bytes 20 | tf_op jit(solution)/shard_map/ppermute | solution.py:15
  11.3 6.1 %collective-permute-start.11 = (s32[1]{0:T(128)}, s32[1]{0:T(128)}, u32[]{:S(2)}, u32[]{:S(2)}) collective-permute-start(s32[1]{0:T(128)} %param.11), channel_id=1, source_target_pairs={{1,0},{2,1},{3,2},{4,3},{5,4},{6,5},{7,6},{8,7},{9,8},{10,9},{11,1... | collective-permute-start | bytes 20 | tf_op jit(solution)/shard_map/ppermute | solution.py:15
  17.3 6.6 %collective-permute-start.12 = (s32[1]{0:T(128)}, s32[1]{0:T(128)}, u32[]{:S(2)}, u32[]{:S(2)}) collective-permute-start(s32[1]{0:T(128)} %param.11), channel_id=1, source_target_pairs={{2,0},{3,1},{4,2},{5,3},{6,4},{7,5},{8,6},{9,7},{10,8},{11,9},{12,... | collective-permute-start | bytes 20 | tf_op jit(solution)/shard_map/ppermute | solution.py:15
  23.9 1.9 collective-permute-start.13
  25.9 5.1 %collective-permute-start.8 = (s32[1]{0:T(128)}, s32[1]{0:T(128)}, u32[]{:S(2)}, u32[]{:S(2)}) collective-permute-start(s32[1]{0:T(128)} %param.11), channel_id=1, source_target_pairs={{29,0},{30,1},{31,2},{0,3},{1,4},{2,5},{3,6},{4,7},{5,8},{6,9},{7,... | collective-permute-start | bytes 20 | tf_op jit(solution)/shard_map/ppermute | solution.py:15
  31.7 0.7 fusion.34
  33.0 0.1 concatenate.27
  33.1 0.1 mul.41
  33.2 0.1 add_convert_fusion
  33.3 0.0 collective-permute-done.10
  33.3 1.9 collective-permute-start.9
  35.2 0.0 collective-permute-done.11
  35.2 1.9 collective-permute-start
  37.2 0.0 collective-permute-done.12
  37.2 2.1 collective-permute-start.1
  39.3 0.0 collective-permute-done.13
  39.3 2.2 %collective-permute-start.2 = (bf16[1,384,384]{2,1,0:T(8,128)(2,1)}, bf16[1,384,384]{2,1,0:T(8,128)(2,1)S(1)}, u32[]{:S(2)}, u32[]{:S(2)}) collective-permute-start(bf16[1,384,384]{2,1,0:T(8,128)(2,1)} %param.12), channel_id=1, source_target_pairs={{31,0},{0,1},{1,2},{2,3},{3,4},{4,5},{5,6},{6,7},{7,8},{8,9},{9,10... | collective-permute-start | bytes 884744 | tf_op jit(solution)/shard_map/ppermute | solution.py:15
  41.5 0.0 collective-permute-done.8
  41.6 2.3 %collective-permute-start.3 = (bf16[1,384,384]{2,1,0:T(8,128)(2,1)}, bf16[1,384,384]{2,1,0:T(8,128)(2,1)S(1)}, u32[]{:S(2)}, u32[]{:S(2)}) collective-permute-start(bf16[1,384,384]{2,1,0:T(8,128)(2,1)} %param.12), channel_id=1, source_target_pairs={{1,0},{2,1},{3,2},{4,3},{5,4},{6,5},{7,6},{8,7},{9,8},{10,9},{11,1... | collective-permute-start | bytes 884744 | tf_op jit(solution)/shard_map/ppermute | solution.py:15
  43.9 0.0 collective-permute-done.9
  43.9 1.8 collective-permute-start.14
  45.7 3.9 %concatenate.28 = s32[7]{0:T(128)S(1)} concatenate(s32[1]{0:T(128)} %collective-permute-done.8, s32[1]{0:T(128)} %collective-permute-done.9, s32[1]{0:T(128)} %collective-permute-done.10, s32[1]{0:T(128)} %copy.19, s32[1]{0:T(128)} %collective-permute-done.11, s32[1]{0:T(128)} %collective-permute-done.12, s32[1]{0:T(128)} %collective-permute-done.13), dimensions={0} | concatenate | bytes 56 | tf_op jit(solution)/shard_map/concatenate | solution.py:48
  49.6 0.6 gather_fusion.1
  50.2 0.7 broadcast_select_fusion.1
  50.9 0.0 collective-permute-done.14
  50.9 1.3 collective-permute-start.15
  52.2 3.4 %collective-permute-done.15 = s32[1]{0:T(128)} collective-permute-done((s32[1]{0:T(128)}, s32[1]{0:T(128)}, u32[]{:S(2)}, u32[]{:S(2)}) %collective-permute-start.15) | collective-permute-done | bytes 36 | tf_op jit(solution)/shard_map/ppermute | solution.py:26
  55.7 6.8 %collective-permute-start.4 = (bf16[1,384,384]{2,1,0:T(8,128)(2,1)}, bf16[1,384,384]{2,1,0:T(8,128)(2,1)S(1)}, u32[]{:S(2)}, u32[]{:S(2)}) collective-permute-start(bf16[1,384,384]{2,1,0:T(8,128)(2,1)} %param.12), channel_id=1, source_target_pairs={{2,0},{3,1},{4,2},{5,3},{6,4},{7,5},{8,6},{9,7},{10,8},{11,9},{12,... | collective-permute-start | bytes 884744 | tf_op jit(solution)/shard_map/ppermute | solution.py:15
  62.4 1.4 pad_add_fusion
  63.8 0.6 compare_convert_fusion
  64.4 0.0 collective-permute-done
  64.4 5.8 %collective-permute-start.5 = (bf16[1,384,384]{2,1,0:T(8,128)(2,1)}, bf16[1,384,384]{2,1,0:T(8,128)(2,1)S(1)}, u32[]{:S(2)}, u32[]{:S(2)}) collective-permute-start(bf16[1,384,384]{2,1,0:T(8,128)(2,1)} %param.12), channel_id=1, source_target_pairs={{3,0},{4,1},{5,2},{6,3},{7,4},{8,5},{9,6},{10,7},{11,8},{12,9},{13... | collective-permute-start | bytes 884744 | tf_op jit(solution)/shard_map/ppermute | solution.py:15
  70.2 0.7 constant_dynamic-update-slice_fusion.6
  70.9 0.0 collective-permute-done.1
  70.9 2.1 collective-permute-start.6
  73.0 0.7 constant_dynamic-update-slice_fusion.5
  73.8 0.0 collective-permute-done.2
  73.8 1.3 collective-permute-start.7
  75.1 0.7 constant_dynamic-update-slice_fusion.4
  75.8 0.0 copy-done
  75.8 0.8 constant_dynamic-update-slice_fusion.3
  76.6 0.0 collective-permute-done.3
  76.6 0.7 constant_dynamic-update-slice_fusion.2
  77.3 0.0 collective-permute-done.4
  77.3 0.8 constant_dynamic-update-slice_fusion.1
  78.1 0.0 collective-permute-done.5
  78.1 0.8 constant_dynamic-update-slice_fusion
  78.8 2.5 %gather_fusion = bf16[6,384,384]{2,1,0:T(8,128)(2,1)S(1)} fusion(bf16[7,384,384]{2,1,0:T(8,128)(2,1)} %constant_dynamic-update-slice_fusion, s32[1024]{0:T(1024)S(1)} %pad_clamp_fusion), kind=kCustom, calls=%fused_computation | custom fusion | bytes 3538968 | tf_op jit(solution)/shard_map/jit(_take)/gather | solution.py:50
  81.4 0.3 broadcast_select_fusion
  81.6 0.0 collective-permute-done.6
  81.7 3.1 %collective-permute-done.7 = bf16[1,384,384]{2,1,0:T(8,128)(2,1)} collective-permute-done((bf16[1,384,384]{2,1,0:T(8,128)(2,1)}, bf16[1,384,384]{2,1,0:T(8,128)(2,1)}, u32[]{:S(2)}, u32[]{:S(2)}) %collective-permute-start.7) | collective-permute-done | bytes 294944 | tf_op jit(solution)/shard_map/ppermute | solution.py:26
  84.8 6.3 %fusion.12 = bf16[8,384,384]{2,1,0:T(8,128)(2,1)} fusion(bf16[2,384,384]{2,1,0:T(8,128)(2,1)} %bitcast.40, bf16[6,384,384]{2,1,0:T(8,128)(2,1)} %bitcast.39, bf16[1,384,384]{2,1,0:T(8,128)(2,1)} %collective-permute-done.7, bf16[1,384,384]{2,1,0:T(8,128)(2,1)} %collective-permute-done.6, bf16[6,384,384]{2,1,0:T(8,128)(2,1)S(1)} %broadcast_select_fusion, ...), kind=kOutput, calls=%fused_computation.16 | convolution fusion | flops 1816657920 | bytes 7372800 | tf_op jit(solution)/shard_map/fc,kfm->kcm/dot_general | solution.py:61
  91.1 0.0 copy-start.1
  91.1 3.3 %copy.10 = bf16[8,384,384]{1,0,2:T(8,128)(2,1)S(1)} copy(bf16[8,384,384]{2,1,0:T(8,128)(2,1)} %fusion.12) | data formatting | bytes 4718592 | tf_op jit(solution)/shard_map/fc,kfm->kcm/dot_general | solution.py:61
  94.4 0.0 copy-done.1
  94.4 3.5 %convert_bitcast_fusion = f32[384,3,2,384]{3,1,2,0:T(4,128)} fusion(bf16[8,384,384]{1,0,2:T(8,128)(2,1)S(1)} %copy.10, f32[8]{0:T(128)S(1)} %add_convert_fusion, f32[8,2]{0,1:T(2,128)S(1)} %copy-done.1, f32[8,3]{0,1:T(4,128)S(1)} %fusion.31), kind=kOutput, calls=%fused_computation.6 | convolution fusion | flops 15040608 | bytes 5898432 | tf_op jit(solution)/shard_map/ksb,kcm->csbm/dot_general | solution.py:78
  97.9 6.2 %copy.8 = f32[384,3,2,384]{0,3,2,1:T(8,128)} copy(f32[384,3,2,384]{3,1,2,0:T(4,128)} %convert_bitcast_fusion) | data formatting | bytes 7077888 | tf_op jit(solution)/shard_map/convert_element_type | solution.py:79
  104.2 3.3 %copy.9 = f32[384,2304]{1,0:T(8,128)S(1)} copy(f32[384,2304]{0,1:T(8,128)} %bitcast.38) | data formatting | bytes 7077888 | tf_op jit(solution)/shard_map/convert_element_type | solution.py:79
  107.5 2.2 %fusion = bf16[768,2304]{1,0:T(8,128)(2,1)} fusion(f32[384,2304]{1,0:T(8,128)S(1)} %copy.9, f32[768]{0:T(1024)S(1)} %mul.42), kind=kLoop, calls=%fused_computation.3 | loop fusion | flops 3538944 | bytes 7080960 | tf_op jit(solution)/shard_map/convert_element_type | solution.py:83
  109.7 0.0 reduce-scatter.2.cloned.1.call-update
  109.7 99.0 %reduce-scatter.2.cloned.1.call-done = bf16[24,2304]{1,0:T(8,128)(2,1)} async-done(((bf16[768,2304]{1,0:T(8,128)(2,1)}), bf16[24,2304]{1,0:T(8,128)(2,1)}) %reduce-scatter.2.cloned.1.call-update) | async-done | bytes 110608 | tf_op jit(solution)/shard_map/reduce_scatter | solution.py:82
  208.7 1.6 convert_element_type.64
  (6 shorter events, 0.0 us)
Async XLA Ops:
  6.5 69.3 %copy-start = (bf16[1,384,384]{2,1,0:T(8,128)(2,1)S(1)}, bf16[1,384,384]{2,1,0:T(8,128)(2,1)}, u32[]{:S(2)}) copy-start(bf16[1,384,384]{2,1,0:T(8,128)(2,1)} %param.12) | copy-start | bytes 884740
  6.5 202.1 %reduce-scatter.2.cloned.1.call-start = ((), (), s32[]{:S(2)}) async-start(), calls=%async_computation.1 | async-start | bytes 3649536 | tf_op jit(solution)/shard_map/reduce_scatter | solution.py:82
  6.5 26.8 %collective-permute-start.10 = (s32[1]{0:T(128)}, s32[1]{0:T(128)}, u32[]{:S(2)}, u32[]{:S(2)}) collective-permute-start(s32[1]{0:T(128)} %param.11), channel_id=1, source_target_pairs={{31,0},{0,1},{1,2},{2,3},{3,4},{4,5},{5,6},{6,7},{7,8},{8,9},{9,10... | collective-permute-start | bytes 20 | tf_op jit(solution)/shard_map/ppermute | solution.py:15
  11.3 24.0 %collective-permute-start.11 = (s32[1]{0:T(128)}, s32[1]{0:T(128)}, u32[]{:S(2)}, u32[]{:S(2)}) collective-permute-start(s32[1]{0:T(128)} %param.11), channel_id=1, source_target_pairs={{1,0},{2,1},{3,2},{4,3},{5,4},{6,5},{7,6},{8,7},{9,8},{10,9},{11,1... | collective-permute-start | bytes 20 | tf_op jit(solution)/shard_map/ppermute | solution.py:15
  17.3 19.8 %collective-permute-start.12 = (s32[1]{0:T(128)}, s32[1]{0:T(128)}, u32[]{:S(2)}, u32[]{:S(2)}) collective-permute-start(s32[1]{0:T(128)} %param.11), channel_id=1, source_target_pairs={{2,0},{3,1},{4,2},{5,3},{6,4},{7,5},{8,6},{9,7},{10,8},{11,9},{12,... | collective-permute-start | bytes 20 | tf_op jit(solution)/shard_map/ppermute | solution.py:15
  23.9 15.4 %collective-permute-start.13 = (s32[1]{0:T(128)}, s32[1]{0:T(128)}, u32[]{:S(2)}, u32[]{:S(2)}) collective-permute-start(s32[1]{0:T(128)} %param.11), channel_id=1, source_target_pairs={{3,0},{4,1},{5,2},{6,3},{7,4},{8,5},{9,6},{10,7},{11,8},{12,9},{13... | collective-permute-start | bytes 20 | tf_op jit(solution)/shard_map/ppermute | solution.py:15
  25.9 15.7 %collective-permute-start.8 = (s32[1]{0:T(128)}, s32[1]{0:T(128)}, u32[]{:S(2)}, u32[]{:S(2)}) collective-permute-start(s32[1]{0:T(128)} %param.11), channel_id=1, source_target_pairs={{29,0},{30,1},{31,2},{0,3},{1,4},{2,5},{3,6},{4,7},{5,8},{6,9},{7,... | collective-permute-start | bytes 20 | tf_op jit(solution)/shard_map/ppermute | solution.py:15
  33.3 10.6 %collective-permute-start.9 = (s32[1]{0:T(128)}, s32[1]{0:T(128)}, u32[]{:S(2)}, u32[]{:S(2)}) collective-permute-start(s32[1]{0:T(128)} %param.11), channel_id=1, source_target_pairs={{30,0},{31,1},{0,2},{1,3},{2,4},{3,5},{4,6},{5,7},{6,8},{7,9},{8,1... | collective-permute-start | bytes 20 | tf_op jit(solution)/shard_map/ppermute | solution.py:15
  35.2 29.2 %collective-permute-start = (bf16[1,384,384]{2,1,0:T(8,128)(2,1)}, bf16[1,384,384]{2,1,0:T(8,128)(2,1)S(1)}, u32[]{:S(2)}, u32[]{:S(2)}) collective-permute-start(bf16[1,384,384]{2,1,0:T(8,128)(2,1)} %param.12), channel_id=1, source_target_pairs={{29,0},{30,1},{31,2},{0,3},{1,4},{2,5},{3,6},{4,7},{5,8},{6,9},{7,... | collective-permute-start | bytes 884744 | tf_op jit(solution)/shard_map/ppermute | solution.py:15
  37.2 33.7 %collective-permute-start.1 = (bf16[1,384,384]{2,1,0:T(8,128)(2,1)}, bf16[1,384,384]{2,1,0:T(8,128)(2,1)S(1)}, u32[]{:S(2)}, u32[]{:S(2)}) collective-permute-start(bf16[1,384,384]{2,1,0:T(8,128)(2,1)} %param.12), channel_id=1, source_target_pairs={{30,0},{31,1},{0,2},{1,3},{2,4},{3,5},{4,6},{5,7},{6,8},{7,9},{8,1... | collective-permute-start | bytes 884744 | tf_op jit(solution)/shard_map/ppermute | solution.py:15
  39.3 34.4 %collective-permute-start.2 = (bf16[1,384,384]{2,1,0:T(8,128)(2,1)}, bf16[1,384,384]{2,1,0:T(8,128)(2,1)S(1)}, u32[]{:S(2)}, u32[]{:S(2)}) collective-permute-start(bf16[1,384,384]{2,1,0:T(8,128)(2,1)} %param.12), channel_id=1, source_target_pairs={{31,0},{0,1},{1,2},{2,3},{3,4},{4,5},{5,6},{6,7},{7,8},{8,9},{9,10... | collective-permute-start | bytes 884744 | tf_op jit(solution)/shard_map/ppermute | solution.py:15
  41.6 35.0 %collective-permute-start.3 = (bf16[1,384,384]{2,1,0:T(8,128)(2,1)}, bf16[1,384,384]{2,1,0:T(8,128)(2,1)S(1)}, u32[]{:S(2)}, u32[]{:S(2)}) collective-permute-start(bf16[1,384,384]{2,1,0:T(8,128)(2,1)} %param.12), channel_id=1, source_target_pairs={{1,0},{2,1},{3,2},{4,3},{5,4},{6,5},{7,6},{8,7},{9,8},{10,9},{11,1... | collective-permute-start | bytes 884744 | tf_op jit(solution)/shard_map/ppermute | solution.py:15
  43.9 7.0 %collective-permute-start.14 = (s32[1]{0:T(128)}, s32[1]{0:T(128)}, u32[]{:S(2)}, u32[]{:S(2)}) collective-permute-start(s32[1]{0:T(128)} %param.11), channel_id=1, source_target_pairs={{0,32},{32,64},{64,96},{96,128},{128,160},{160,192},{192,224},{224... | collective-permute-start | bytes 20 | tf_op jit(solution)/shard_map/ppermute | solution.py:25
  50.9 4.7 %collective-permute-start.15 = (s32[1]{0:T(128)}, s32[1]{0:T(128)}, u32[]{:S(2)}, u32[]{:S(2)}) collective-permute-start(s32[1]{0:T(128)} %param.11), channel_id=1, source_target_pairs={{32,0},{64,32},{96,64},{128,96},{160,128},{192,160},{224,192},{256... | collective-permute-start | bytes 20 | tf_op jit(solution)/shard_map/ppermute | solution.py:26
  55.7 21.6 %collective-permute-start.4 = (bf16[1,384,384]{2,1,0:T(8,128)(2,1)}, bf16[1,384,384]{2,1,0:T(8,128)(2,1)S(1)}, u32[]{:S(2)}, u32[]{:S(2)}) collective-permute-start(bf16[1,384,384]{2,1,0:T(8,128)(2,1)} %param.12), channel_id=1, source_target_pairs={{2,0},{3,1},{4,2},{5,3},{6,4},{7,5},{8,6},{9,7},{10,8},{11,9},{12,... | collective-permute-start | bytes 884744 | tf_op jit(solution)/shard_map/ppermute | solution.py:15
  64.4 13.7 %collective-permute-start.5 = (bf16[1,384,384]{2,1,0:T(8,128)(2,1)}, bf16[1,384,384]{2,1,0:T(8,128)(2,1)S(1)}, u32[]{:S(2)}, u32[]{:S(2)}) collective-permute-start(bf16[1,384,384]{2,1,0:T(8,128)(2,1)} %param.12), channel_id=1, source_target_pairs={{3,0},{4,1},{5,2},{6,3},{7,4},{8,5},{9,6},{10,7},{11,8},{12,9},{13... | collective-permute-start | bytes 884744 | tf_op jit(solution)/shard_map/ppermute | solution.py:15
  70.9 10.8 %collective-permute-start.6 = (bf16[1,384,384]{2,1,0:T(8,128)(2,1)}, bf16[1,384,384]{2,1,0:T(8,128)(2,1)}, u32[]{:S(2)}, u32[]{:S(2)}) collective-permute-start(bf16[1,384,384]{2,1,0:T(8,128)(2,1)} %param.12), channel_id=1, source_target_pairs={{0,32},{32,64},{64,96},{96,128},{128,160},{160,192},{192,224},{224... | collective-permute-start | bytes 884744 | tf_op jit(solution)/shard_map/ppermute | solution.py:25
  73.8 11.0 %collective-permute-start.7 = (bf16[1,384,384]{2,1,0:T(8,128)(2,1)}, bf16[1,384,384]{2,1,0:T(8,128)(2,1)}, u32[]{:S(2)}, u32[]{:S(2)}) collective-permute-start(bf16[1,384,384]{2,1,0:T(8,128)(2,1)} %param.12), channel_id=1, source_target_pairs={{32,0},{64,32},{96,64},{128,96},{160,128},{192,160},{224,192},{256... | collective-permute-start | bytes 884744 | tf_op jit(solution)/shard_map/ppermute | solution.py:26
  91.1 3.3 %copy-start.1 = (f32[8,2]{0,1:T(2,128)S(1)}, f32[8,2]{0,1:T(2,128)}, u32[]{:S(2)}) copy-start(f32[8,2]{0,1:T(2,128)} %compare_convert_fusion) | copy-start | bytes 196
Sparse Core Ops, SparseCore 0:
  109.8 98.7 reduce-scatter.1
where the time goes:
time: 219 us; the launch traced here: 217 us
  waiting for transfers between devices  106 us (48%)
  starting transfers between devices  54 us (25%)
  local copies, waits for them, and re-layouts  25.3 us (12%)
  between operations  14.9 us (7%)
  matrix products  9.8 us (4%)
  other arithmetic  7.47 us (3%)
    reduce_scatter x1, waiting for transfers between devices, on_device(): lax.psum_scatter(spread.astype(jnp.bfloat16), 'dev', scatter_dimension=0,...  99 us
    ppermute x12, starting transfers between devices, passed_along(): return lax.ppermute(block, axis, route)  47.4 us
    convert_element_type x2, local copies, waits for them, and re-layouts, on_device(): partial_value = partial_value.astype(jnp.bfloat16).astype(jnp.float32)  9.53 us
    ppermute x2, waiting for transfers between devices, extended(): after = lax.ppermute(initial, axis, down)  6.57 us
    dot_general x1, matrix products, on_device(): jnp.einsum('fc,kfm->kcm', prolong[0], qmat, preferred_element_type=jnp.fl...  6.32 us
    unnamed x10, local copies, waits for them, and re-layouts  4.47 us
  transfers between devices with their start and end apart: 17, of which 3 were waited for; matrix products, arithmetic and copies ran while one was open for 7% of the time, Pallas kernels for 0%

commit v1 on v0

v1 whole, which is shorter than its diff:
```python
import jax
import jax.numpy as jnp
from jax import lax
from jax.experimental import pallas as pl
from jax.experimental.pallas import tpu as pltpu
from jax.sharding import PartitionSpec as P

NB = 384
SLOTS = 6
TAIL = 16
ROWS = NB + TAIL
CUT = 192
SIDE = 4
BAND = 48
HALF = 3 * NB
MESH = pl.DeviceIdType.MESH
BF = jnp.bfloat16
F32 = jnp.float32


def kernel(
    cols, live, agg, stiff_rows, stiff_iface, prolong, out,
    win, bbuf, pt, tbuf, acc, xbuf, pbuf, dense, got_far, got_near, gather, got_last, fin, got_fin,
    load_sem, send_sem, recv_sem, send2, recv2,
):
    g = lax.axis_index("grp")
    d = lax.axis_index("dev")
    groups = lax.axis_size("grp")
    devs = lax.axis_size("dev")
    k = lax.rem(d, 2)
    c = d // 2
    chips = devs // 2
    x = c // SIDE
    y = lax.rem(c, SIDE)
    own = 2 + k

    def at(cx, cy, core):
        return (g, (lax.rem(cx, SIDE) * SIDE + lax.rem(cy, SIDE)) * 2 + core)

    partner = (g, c * 2 + 1 - k)
    nxt = (g, lax.rem(c + 1, chips) * 2 + k)
    prv = (g, lax.rem(c + chips - 1, chips) * 2 + k)
    far = (g, lax.rem(c + chips + 2 * k - 1, chips) * 2 + 1 - k)
    above = (lax.rem(g + 1, groups), d)
    below = (lax.rem(g + groups - 1, groups), d)
    fx, fy = 1 - k, k
    first_up = at(x + fx, y + fy, k)
    first_down = at(x + 3 * fx, y + 3 * fy, k)
    second = [at(x + s * fy, y + s * fx, k) for s in (1, 2, 3)]

    load_p = pltpu.make_async_copy(prolong.at[0], win.at[own, pl.ds(0, NB)], load_sem.at[0])
    load_b = pltpu.make_async_copy(stiff_rows.at[0], bbuf.at[pl.ds(0, SLOTS)], load_sem.at[1])
    load_i = pltpu.make_async_copy(stiff_iface.at[0], bbuf.at[pl.ds(SLOTS, 2)], load_sem.at[2])
    load_p.start()
    win[own, NB:ROWS, :] = jnp.full((TAIL, NB), agg[0].astype(F32), F32).astype(BF)

    barrier = pltpu.get_barrier_semaphore()
    peers = [partner, nxt, prv, far, above, below, first_up, first_down] + second
    for peer in peers:
        pl.semaphore_signal(barrier, inc=1, device_id=peer, device_id_type=MESH)
    load_p.wait()
    load_b.start()
    load_i.start()
    pl.semaphore_wait(barrier, len(peers))

    parts = (pl.ds(0, CUT), pl.ds(CUT, ROWS - CUT))

    def remote(src, dst, sems, rems, peer):
        return pltpu.make_async_remote_copy(
            src_ref=src, dst_ref=dst, send_sem=sems, recv_sem=rems, device_id=peer, device_id_type=MESH
        )

    sent = []

    def go(copy):
        copy.start()
        sent.append(copy)

    def move(src_slot, dst_slot, part, number, peer):
        return remote(
            win.at[src_slot, parts[part]], win.at[dst_slot, parts[part]],
            send_sem.at[number], recv_sem.at[dst_slot, part], peer,
        )

    def arrived(slot, part):
        move(slot, slot, part, 0, partner).wait_recv()

    for part in range(2):
        go(move(own, k, part, part, nxt))
        go(move(own, 4 + k, part, 2 + part, prv))
    for part in range(2):
        go(move(own, 7, part, 4 + part, above))
        go(move(own, 8, part, 6 + part, below))
        go(move(own, own, part, 8 + part, partner))

    pt[...] = win[own, 0:NB, :].astype(F32).T.astype(BF)
    load_b.wait()
    load_i.wait()

    @pl.loop(0, SLOTS + 2)
    def _(index):
        tbuf[index] = jnp.dot(pt[...], bbuf[index], preferred_element_type=F32).astype(BF)

    base = 2 * c
    live_now = live[0]
    slot_of = []
    for index in range(SLOTS):
        rel = lax.rem(cols[0, index] - base + 2 + 2 * devs, devs)
        slot_of.append(jnp.minimum(rel, 6))

    def row_of(slot):
        return win[slot, NB:ROWS, :].astype(F32)[0:1, :]

    def take_in(slot, fresh=False):
        index = jnp.int32(0)
        weight = jnp.int32(0)
        for number in range(SLOTS):
            hit = (slot_of[number] == slot).astype(jnp.int32)
            index = index + hit * number
            weight = weight + hit * (number < live_now).astype(jnp.int32)
        index = jnp.minimum(index, SLOTS - 1)
        scale = weight.astype(F32)
        high = row_of(slot) * scale
        low = scale - high
        value = jnp.dot(tbuf[index], win[slot, 0:NB, :], preferred_element_type=F32)
        if fresh:
            acc[1] = value * low
            acc[2] = value * high
        else:
            acc[1] += value * low
            acc[2] += value * high

    take_in(own, True)
    for part in range(2):
        arrived(3 - k, part)
    take_in(3 - k)

    relay_from = 4 - 3 * k
    for part in range(2):
        arrived(k, part)
        arrived(4 + k, part)
        go(move(relay_from, 6, part, 10 + part, far))
        go(move(k, k, part, 12 + part, partner))
        go(move(4 + k, 4 + k, part, 14 + part, partner))
    take_in(k)
    take_in(4 + k)

    for slot, index, place, weight in (
        (7, SLOTS, 0, (g > 0).astype(F32)),
        (8, SLOTS + 1, 3, (g < groups - 1).astype(F32)),
    ):
        for part in range(2):
            arrived(slot, part)
        value = jnp.dot(tbuf[index], win[slot, 0:NB, :], preferred_element_type=F32) * weight
        acc[place] = value
        xbuf[place, 0:NB, :] = value.astype(BF)
        xbuf[place, NB:ROWS, :] = win[slot, NB:ROWS, :]

    for slot in (1 - k, 5 - k, 6):
        for part in range(2):
            arrived(slot, part)
        take_in(slot)

    for place in (1, 2):
        xbuf[place, 0:NB, :] = acc[place].astype(BF)
        xbuf[place, NB:ROWS, :] = jnp.zeros((TAIL, NB), BF)

    def second_copy(src, dst, number, peer):
        return remote(src, dst, send2.at[number], recv2.at[number], peer)

    pair = second_copy(xbuf.at[pl.ds(2 * (1 - k), 2)], pbuf, 0, partner)
    go(pair)
    pair.wait_recv()

    edge_mine, mid_mine = 3 * k, 1 + k
    edge_theirs, mid_theirs = k, 1 - k
    mine_row = row_of(own)
    their_row = row_of(3 - k)
    edge_row = xbuf[edge_mine, NB:ROWS, :].astype(F32)[0:1, :]
    edge_row2 = pbuf[edge_theirs, NB:ROWS, :].astype(F32)[0:1, :]

    @pl.loop(0, 2 * SIDE)
    def _(block):
        rows = pl.ds(pl.multiple_of(block * BAND, BAND), BAND)
        e1 = acc[edge_mine, rows, :]
        m1 = acc[mid_mine, rows, :]
        e2 = pbuf[edge_theirs, rows, :].astype(F32)
        m2 = pbuf[mid_theirs, rows, :].astype(F32)
        for coarse in range(2):
            w1 = mine_row if coarse else 1.0 - mine_row
            w2 = their_row if coarse else 1.0 - their_row
            to_x = 2 * coarse + block // SIDE
            to_y = lax.rem(block, SIDE)
            u = to_x * fx + to_y * fy
            v = to_x * fy + to_y * fx
            dense[u, v, :, 0:NB] = (e1 * (w1 * (1.0 - edge_row)) + e2 * (w2 * (1.0 - edge_row2))).astype(BF)
            dense[u, v, :, NB:2 * NB] = (e1 * (w1 * edge_row) + e2 * (w2 * edge_row2)).astype(BF)
            dense[u, v, :, 2 * NB:HALF] = (m1 * w1 + m2 * w2).astype(BF)

    me = x * fx + y * fy
    up = lax.rem(me + 1, SIDE)
    opposite = lax.rem(me + 2, SIDE)
    down = lax.rem(me + 3, SIDE)
    lo, hi = pl.ds(0, 2), pl.ds(2, 2)
    far_up = second_copy(dense.at[opposite, lo], got_far.at[0], 1, first_up)
    far_down = second_copy(dense.at[opposite, hi], got_far.at[1], 2, first_down)
    go(far_up)
    go(far_down)
    up_hi = second_copy(dense.at[up, hi], got_near.at[0, hi], 3, first_up)
    down_lo = second_copy(dense.at[down, lo], got_near.at[1, lo], 4, first_down)
    go(up_hi)
    go(down_lo)
    far_up.wait_recv()
    for v in range(2):
        dense[up, v] = (dense[up, v].astype(F32) + got_far[0, v].astype(F32)).astype(BF)
    up_lo = second_copy(dense.at[up, lo], got_near.at[0, lo], 5, first_up)
    go(up_lo)
    far_down.wait_recv()
    for v in range(2):
        dense[down, 2 + v] = (dense[down, 2 + v].astype(F32) + got_far[1, v].astype(F32)).astype(BF)
    down_hi = second_copy(dense.at[down, hi], got_near.at[1, hi], 6, first_down)
    go(down_hi)
    for copy in (up_hi, down_lo, up_lo, down_hi):
        copy.wait_recv()

    @pl.loop(0, SIDE)
    def _(v):
        gather[v] = (
            dense[me, v].astype(F32) + got_near[0, v].astype(F32) + got_near[1, v].astype(F32)
        ).astype(BF)

    mine = x * fy + y * fx
    lasts = []
    for step in (2, 1, 3):
        copy = second_copy(
            gather.at[lax.rem(mine + step, SIDE)], got_last.at[step - 1], 6 + step, second[step - 1]
        )
        go(copy)
        lasts.append(copy)
    for copy in lasts:
        copy.wait_recv()
    fin[...] = (
        gather[mine].astype(F32) + got_last[0].astype(F32) + got_last[1].astype(F32) + got_last[2].astype(F32)
    ).reshape(2, BAND // 2, HALF)

    swap = second_copy(fin.at[1 - k], got_fin, 10, partner)
    go(swap)

    def place_half(side, ref):
        edge_at = side * (HALF + NB)
        mid_at = 2 * NB + side * NB
        out[:, pl.ds(pl.multiple_of(edge_at, 128), 2 * NB)] = ref[:, 0:2 * NB]
        out[:, pl.ds(pl.multiple_of(mid_at, 128), NB)] = ref[:, 2 * NB:HALF]

    place_half(k, fin.at[k])
    swap.wait_recv()
    place_half(1 - k, got_fin)
    for copy in sent:
        copy.wait_send()


def on_device(stiff_rows, stiff_iface, columns, live_count, aggregate, prolong):
    smem = pl.BlockSpec(memory_space=pltpu.SMEM)
    anywhere = pl.BlockSpec(memory_space=pl.ANY)
    return pl.pallas_call(
        kernel,
        out_shape=jax.ShapeDtypeStruct((BAND // 2, 2 * HALF), F32),
        in_specs=[smem, smem, smem, anywhere, anywhere, anywhere],
        out_specs=pl.BlockSpec(memory_space=pltpu.VMEM),
        scratch_shapes=[
            pltpu.VMEM((9, ROWS, NB), BF),
            pltpu.VMEM((SLOTS + 2, NB, NB), BF),
            pltpu.VMEM((NB, NB), BF),
            pltpu.VMEM((SLOTS + 2, NB, NB), BF),
            pltpu.VMEM((4, NB, NB), F32),
            pltpu.VMEM((4, ROWS, NB), BF),
            pltpu.VMEM((2, ROWS, NB), BF),
            pltpu.VMEM((SIDE, SIDE, BAND, HALF), BF),
            pltpu.VMEM((2, 2, BAND, HALF), BF),
            pltpu.VMEM((2, SIDE, BAND, HALF), BF),
            pltpu.VMEM((SIDE, BAND, HALF), BF),
            pltpu.VMEM((3, BAND, HALF), BF),
            pltpu.VMEM((2, BAND // 2, HALF), F32),
            pltpu.VMEM((BAND // 2, HALF), F32),
            pltpu.SemaphoreType.DMA((3,)),
            pltpu.SemaphoreType.DMA((16,)),
            pltpu.SemaphoreType.DMA((9, 2)),
            pltpu.SemaphoreType.DMA((11,)),
            pltpu.SemaphoreType.DMA((11,)),
        ],
        compiler_params=pltpu.CompilerParams(
            collective_id=0, has_side_effects=True, vmem_limit_bytes=60 * 1024 * 1024
        ),
        name="coarse",
    )(columns, live_count, aggregate, stiff_rows, stiff_iface, prolong)


def solution(mesh):
    in_specs = (
        P(("grp", "dev"), None, None, None),
        P(("grp", "dev"), None, None, None),
        P(("grp", "dev"), None),
        P(("grp", "dev")),
        P(("grp", "dev")),
        P(("grp", "dev"), None, None),
    )
    out_specs = P(("grp", "dev"), None)
    return jax.shard_map(
        on_device, mesh=mesh, in_specs=in_specs, out_specs=out_specs, check_vma=False
    )
```

time: 219 us -> 55.9 us (0.26)
  waiting for transfers between devices: 106 us -> 0 us
  starting transfers between devices: 54 us -> 0 us
  Pallas kernels: 0 us -> 52.7 us
  local copies, waits for them, and re-layouts: 25.3 us -> 1.64 us
  between operations: 14.9 us -> 1.3 us
  matrix products: 9.8 us -> 0 us
  other arithmetic: 7.47 us -> 0 us
    reduce_scatter x1 -> x0, waiting for transfers between devices: 99 us -> none  [on_device(): lax.psum_scatter(spread.astype(jnp.bfloat16), 'dev', scatter_dimension=0,...]
    ppermute x16 -> x0, starting transfers between devices: 54 us -> none  [the longest x12 47.4 us: passed_along(): return lax.ppermute(block, axis, route)]
    pallas_call x0 -> x1, Pallas kernels: none -> 52.7 us  [on_device(): pl.pallas_call(kernel, out_shape=jax.ShapeDtypeStruct((BAND // 2, 2 * HAL...]
    dot_general x2 -> x0, matrix products: 9.8 us -> none  [the longest x1 6.32 us: on_device(): jnp.einsum('fc,kfm->kcm', prolong[0], qmat, preferred_element_type=jnp.fl...]
    convert_element_type x2 -> x0, local copies, waits for them, and re-layouts: 9.53 us -> none  [on_device(): partial_value = partial_value.astype(jnp.bfloat16).astype(jnp.float32)]
    ppermute x16 -> x0, waiting for transfers between devices: 6.61 us -> none  [the longest x2 6.57 us: extended(): after = lax.ppermute(initial, axis, down)]
    concatenate x3 -> x0, local copies, waits for them, and re-layouts: 4.74 us -> none  [the longest x1 3.89 us: on_device(): window_aggs = jnp.concatenate(agg_list, axis=0)]
    convert_element_type x5 -> x0, other arithmetic: 4.37 us -> none  [the longest x1 2.2 us: on_device(): spread.astype(jnp.bfloat16)]
  transfers between devices with their start and end apart: 17 -> 0, of which waited for: 3 -> 0; matrix products, arithmetic and copies ran while one was open for 7% -> 0% of each run, Pallas kernels for 0% -> 0%
where the time goes in v1:
time: 55.9 us; the launch traced here: 55.7 us
  Pallas kernels  52.7 us (94%)
  local copies, waits for them, and re-layouts  1.64 us (3%)
  between operations  1.3 us (2%)
    pallas_call x1, Pallas kernels, on_device(): pl.pallas_call(kernel, out_shape=jax.ShapeDtypeStruct((BAND // 2, 2 * HAL...  52.7 us
    unnamed x1, local copies, waits for them, and re-layouts  1.64 us

profile of v1, /device:TPU:1, one launch (start us, length us, event | category | flops | bytes accessed | tf_op | source)
XLA Modules:
  0.0 55.7 jit_solution(2390944066641851031)
XLA Ops:
  1.3 52.7 %coarse.1 = f32[24,2304]{1,0:T(8,128)} custom-call(s32[1,6]{1,0:T(1,128)} %cols.1, s32[1]{0:T(128)S(6)} %copy.8.live, s32[1]{0:T(128)S(6)} %copy.9.agg, bf16[1,6,384,384]{3,2,1,0:T(8,128)(2,1)} %stiff_rows.1, bf16[1,2,384,384]{3,2,1,0:T(8,128)(2,1)} %stiff_iface.1, bf16[1,384,384]{2,1,0:T(8,128)(2,1)} %prolong.1), custom_call_target="tpu_custom_call" | custom-call | tf_op jit(solution)/shard_map/coarse/pallas_call | solution.py:265
  54.0 1.6 %copy.10 = f32[24,2304]{1,0:T(8,128)} copy(f32[24,2304]{1,0:T(8,128)} %coarse.1) | data formatting | bytes 442368

commit v2 on v1

v2 whole, which is shorter than its diff:
```python
import jax
import jax.numpy as jnp
from jax import lax
from jax.experimental import pallas as pl
from jax.experimental.pallas import tpu as pltpu
from jax.sharding import PartitionSpec as P

NB = 384
SLOTS = 6
TAIL = 16
ROWS = NB + TAIL
CUT = 192
SIDE = 4
BAND = 48
HALF = 3 * NB
MESH = pl.DeviceIdType.MESH
BF = jnp.bfloat16
F32 = jnp.float32


def kernel(
    cols, live, agg, stiff_rows, stiff_iface, prolong, out,
    win, bbuf, pt, tbuf, acc, acc_e, xe, pe, xm, pm,
    dense_e, far_e, near_e, sum_e, last_e, dense_m, far_m, near_m, sum_m, last_m, fin, got_fin,
    load_sem, send_sem, recv_sem, send2, recv2,
):
    g = lax.axis_index("grp")
    d = lax.axis_index("dev")
    groups = lax.axis_size("grp")
    devs = lax.axis_size("dev")
    k = lax.rem(d, 2)
    c = d // 2
    chips = devs // 2
    x = c // SIDE
    y = lax.rem(c, SIDE)
    own = 2 + k

    def at(cx, cy):
        return (g, (lax.rem(cx, SIDE) * SIDE + lax.rem(cy, SIDE)) * 2 + k)

    partner = (g, c * 2 + 1 - k)
    nxt = (g, lax.rem(c + 1, chips) * 2 + k)
    prv = (g, lax.rem(c + chips - 1, chips) * 2 + k)
    far = (g, lax.rem(c + chips + 2 * k - 1, chips) * 2 + 1 - k)
    above = (jnp.minimum(g + 1, groups - 1), d)
    below = (jnp.maximum(g - 1, 0), d)
    has_above = g < groups - 1
    has_below = g > 0
    along_x = [at(x + s, y) for s in (1, 2, 3)]
    along_y = [at(x, y + s) for s in (1, 2, 3)]

    load_p = pltpu.make_async_copy(prolong.at[0], win.at[own, pl.ds(0, NB)], load_sem.at[0])
    load_b = pltpu.make_async_copy(stiff_rows.at[0], bbuf.at[pl.ds(0, SLOTS)], load_sem.at[1])
    load_i = pltpu.make_async_copy(stiff_iface.at[0], bbuf.at[pl.ds(SLOTS, 2)], load_sem.at[2])
    load_p.start()

    barrier = pltpu.get_barrier_semaphore()
    peers = [partner, nxt, prv, far] + along_x + along_y

    @pl.when(has_above)
    def _():
        pl.semaphore_signal(barrier, inc=1, device_id=above, device_id_type=MESH)

    @pl.when(has_below)
    def _():
        pl.semaphore_signal(barrier, inc=1, device_id=below, device_id_type=MESH)

    for peer in peers:
        pl.semaphore_signal(barrier, inc=1, device_id=peer, device_id_type=MESH)
    win[own, NB:ROWS, :] = jnp.full((TAIL, NB), agg[0].astype(F32), F32).astype(BF)

    @pl.when(jnp.logical_not(has_below))
    def _():
        win[7] = jnp.zeros((ROWS, NB), BF)

    @pl.when(jnp.logical_not(has_above))
    def _():
        win[8] = jnp.zeros((ROWS, NB), BF)

    load_p.wait()
    load_b.start()
    load_i.start()
    pl.semaphore_wait(barrier, len(peers) + has_above.astype(jnp.int32) + has_below.astype(jnp.int32))

    parts = (pl.ds(0, CUT), pl.ds(CUT, ROWS - CUT))

    def remote(src, dst, sems, rems, peer):
        return pltpu.make_async_remote_copy(
            src_ref=src, dst_ref=dst, send_sem=sems, recv_sem=rems, device_id=peer, device_id_type=MESH
        )

    sent = []

    def go(copy):
        copy.start()
        sent.append(copy)
        return copy

    def move(src_slot, dst_slot, part, number, peer):
        return remote(
            win.at[src_slot, parts[part]], win.at[dst_slot, parts[part]],
            send_sem.at[number], recv_sem.at[dst_slot, part], peer,
        )

    def arrived(slot, part):
        move(slot, slot, part, 0, partner).wait_recv()

    to_above = remote(win.at[own], win.at[7], send_sem.at[4], recv_sem.at[7, 0], above)
    to_below = remote(win.at[own], win.at[8], send_sem.at[5], recv_sem.at[8, 0], below)
    for part in range(2):
        go(move(own, k, part, part, nxt))
        go(move(own, 4 + k, part, 2 + part, prv))

    @pl.when(has_above)
    def _():
        to_above.start()

    @pl.when(has_below)
    def _():
        to_below.start()

    for part in range(2):
        go(move(own, own, part, 8 + part, partner))

    pt[...] = win[own, 0:NB, :].astype(F32).T.astype(BF)
    load_b.wait()
    load_i.wait()

    @pl.loop(0, SLOTS + 2)
    def _(index):
        tbuf[index] = jnp.dot(pt[...], bbuf[index], preferred_element_type=F32).astype(BF)

    base = 2 * c
    live_now = live[0]
    slot_of = []
    for index in range(SLOTS):
        rel = lax.rem(cols[0, index] - base + 2 + 2 * devs, devs)
        slot_of.append(jnp.minimum(rel, 6))

    def row_of(slot):
        return win[slot, NB:ROWS, :].astype(F32)[0:1, :]

    def take_in(slot, fresh=False):
        index = jnp.int32(0)
        weight = jnp.int32(0)
        for number in range(SLOTS):
            hit = (slot_of[number] == slot).astype(jnp.int32)
            index = index + hit * number
            weight = weight + hit * (number < live_now).astype(jnp.int32)
        index = jnp.minimum(index, SLOTS - 1)
        scale = weight.astype(F32)
        high = row_of(slot) * scale
        low = scale - high
        value = jnp.dot(tbuf[index], win[slot, 0:NB, :], preferred_element_type=F32)
        if fresh:
            acc[0] = value * low
            acc[1] = value * high
        else:
            acc[0] += value * low
            acc[1] += value * high

    take_in(own, True)
    for part in range(2):
        arrived(3 - k, part)
    take_in(3 - k)

    relay_from = 4 - 3 * k
    for part in range(2):
        arrived(relay_from, part)
        go(move(relay_from, 6, part, 10 + part, far))
        arrived(5 * k, part)
        go(move(k, k, part, 12 + part, partner))
        go(move(4 + k, 4 + k, part, 14 + part, partner))

    @pl.when(has_below)
    def _():
        to_above.wait_recv()

    @pl.when(has_above)
    def _():
        to_below.wait_recv()

    def second_copy(src, dst, number, peer):
        return remote(src, dst, send2.at[number], recv2.at[number], peer)

    xe[0:NB, :] = jnp.dot(tbuf[7 - k], win[8 - k, 0:NB, :], preferred_element_type=F32).astype(BF)
    xe[NB:ROWS, :] = win[8 - k, NB:ROWS, :]
    pair_e = go(second_copy(xe, pe, 0, partner))
    acc_e[...] = jnp.dot(tbuf[6 + k], win[7 + k, 0:NB, :], preferred_element_type=F32)
    mine_row = row_of(own)
    their_row = row_of(3 - k)
    edge_row = row_of(7 + k)
    pair_e.wait_recv()
    edge_row2 = pe[NB:ROWS, :].astype(F32)[0:1, :]

    @pl.loop(0, 2 * SIDE)
    def _(block):
        rows = pl.ds(pl.multiple_of(block * BAND, BAND), BAND)
        e1 = acc_e[rows, :]
        e2 = pe[rows, :].astype(F32)
        for coarse in range(2):
            w1 = mine_row if coarse else 1.0 - mine_row
            w2 = their_row if coarse else 1.0 - their_row
            u = 2 * coarse + block // SIDE
            v = lax.rem(block, SIDE)
            dense_e[u, v, :, 0:NB] = (e1 * (w1 * (1.0 - edge_row)) + e2 * (w2 * (1.0 - edge_row2))).astype(BF)
            dense_e[u, v, :, NB:2 * NB] = (e1 * (w1 * edge_row) + e2 * (w2 * edge_row2)).astype(BF)

    lo, hi = pl.ds(0, 2), pl.ds(2, 2)

    class Ring:
        def __init__(self, buf, far_buf, near_buf, total, me, line, number):
            self.buf, self.far, self.near, self.total, self.me = buf, far_buf, near_buf, total, me
            self.plus, self.minus, self.number = line[0], line[2], number
            self.up = lax.rem(me + 1, SIDE)
            self.opposite = lax.rem(me + 2, SIDE)
            self.down = lax.rem(me + 3, SIDE)

        def begin(self):
            n, buf = self.number, self.buf
            self.first = [
                go(second_copy(buf.at[self.opposite, lo], self.far.at[0], n, self.plus)),
                go(second_copy(buf.at[self.opposite, hi], self.far.at[1], n + 1, self.minus)),
            ]
            self.rest = [
                go(second_copy(buf.at[self.up, hi], self.near.at[0, hi], n + 2, self.plus)),
                go(second_copy(buf.at[self.down, lo], self.near.at[1, lo], n + 3, self.minus)),
            ]

        def relay(self):
            n, buf = self.number, self.buf
            self.first[0].wait_recv()
            for v in range(2):
                buf[self.up, v] = (buf[self.up, v].astype(F32) + self.far[0, v].astype(F32)).astype(BF)
            self.rest.append(go(second_copy(buf.at[self.up, lo], self.near.at[0, lo], n + 4, self.plus)))
            self.first[1].wait_recv()
            for v in range(2):
                buf[self.down, 2 + v] = (
                    buf[self.down, 2 + v].astype(F32) + self.far[1, v].astype(F32)
                ).astype(BF)
            self.rest.append(go(second_copy(buf.at[self.down, hi], self.near.at[1, hi], n + 5, self.minus)))

        def end(self):
            for copy in self.rest:
                copy.wait_recv()

            @pl.loop(0, SIDE)
            def _(v):
                self.total[v] = (
                    self.buf[self.me, v].astype(F32) + self.near[0, v].astype(F32) + self.near[1, v].astype(F32)
                ).astype(BF)

    ring_e = Ring(dense_e, far_e, near_e, sum_e, x, along_x, 2)
    ring_m = Ring(dense_m, far_m, near_m, sum_m, y, along_y, 8)
    ring_e.begin()

    take_in(k)
    take_in(4 + k)
    for slot in (1 - k, 5 - k, 6):
        for part in range(2):
            arrived(slot, part)
        take_in(slot)
    xm[...] = acc[1 - k].astype(BF)
    pair_m = go(second_copy(xm, pm, 1, partner))
    ring_e.relay()
    pair_m.wait_recv()

    @pl.loop(0, 2 * SIDE)
    def _(block):
        rows = pl.ds(pl.multiple_of(block * BAND, BAND), BAND)
        m1 = acc[k, rows, :]
        m2 = pm[rows, :].astype(F32)
        for coarse in range(2):
            w1 = mine_row if coarse else 1.0 - mine_row
            w2 = their_row if coarse else 1.0 - their_row
            dense_m[lax.rem(block, SIDE), 2 * coarse + block // SIDE] = (m1 * w1 + m2 * w2).astype(BF)

    ring_m.begin()

    def spread(total, last, me, line, number):
        return [
            go(second_copy(total.at[lax.rem(me + step, SIDE)], last.at[step - 1], number + step, line[step - 1]))
            for step in (2, 1, 3)
        ]

    ring_e.end()
    lasts = spread(sum_e, last_e, y, along_y, 13)
    ring_m.relay()
    ring_m.end()
    lasts = lasts + spread(sum_m, last_m, x, along_x, 16)
    for copy in lasts:
        copy.wait_recv()

    def closed(total, last, me, width):
        value = total[me].astype(F32)
        for number in range(3):
            value = value + last[number].astype(F32)
        return value.reshape(2, BAND // 2, width)

    fin[:, :, 0:2 * NB] = closed(sum_e, last_e, y, 2 * NB)
    fin[:, :, 2 * NB:HALF] = closed(sum_m, last_m, x, NB)
    swap = go(second_copy(fin.at[1 - k], got_fin, 20, partner))

    def place_half(side, ref):
        edge_at = side * (HALF + NB)
        mid_at = 2 * NB + side * NB
        out[:, pl.ds(pl.multiple_of(edge_at, 128), 2 * NB)] = ref[:, 0:2 * NB]
        out[:, pl.ds(pl.multiple_of(mid_at, 128), NB)] = ref[:, 2 * NB:HALF]

    place_half(k, fin.at[k])
    swap.wait_recv()
    place_half(1 - k, got_fin)

    @pl.when(has_above)
    def _():
        to_above.wait_send()

    @pl.when(has_below)
    def _():
        to_below.wait_send()

    for copy in sent:
        copy.wait_send()


def ring_buffers(width):
    return [
        pltpu.VMEM((SIDE, SIDE, BAND, width), BF),
        pltpu.VMEM((2, 2, BAND, width), BF),
        pltpu.VMEM((2, SIDE, BAND, width), BF),
        pltpu.VMEM((SIDE, BAND, width), BF),
        pltpu.VMEM((3, BAND, width), BF),
    ]


def on_device(stiff_rows, stiff_iface, columns, live_count, aggregate, prolong):
    smem = pl.BlockSpec(memory_space=pltpu.SMEM)
    anywhere = pl.BlockSpec(memory_space=pl.ANY)
    return pl.pallas_call(
        kernel,
        out_shape=jax.ShapeDtypeStruct((BAND // 2, 2 * HALF), F32),
        in_specs=[smem, smem, smem, anywhere, anywhere, anywhere],
        out_specs=pl.BlockSpec(memory_space=pltpu.VMEM),
        scratch_shapes=[
            pltpu.VMEM((9, ROWS, NB), BF),
            pltpu.VMEM((SLOTS + 2, NB, NB), BF),
            pltpu.VMEM((NB, NB), BF),
            pltpu.VMEM((SLOTS + 2, NB, NB), BF),
            pltpu.VMEM((2, NB, NB), F32),
            pltpu.VMEM((NB, NB), F32),
            pltpu.VMEM((ROWS, NB), BF),
            pltpu.VMEM((ROWS, NB), BF),
            pltpu.VMEM((NB, NB), BF),
            pltpu.VMEM((NB, NB), BF),
            *ring_buffers(2 * NB),
            *ring_buffers(NB),
            pltpu.VMEM((2, BAND // 2, HALF), F32),
            pltpu.VMEM((BAND // 2, HALF), F32),
            pltpu.SemaphoreType.DMA((3,)),
            pltpu.SemaphoreType.DMA((16,)),
            pltpu.SemaphoreType.DMA((9, 2)),
            pltpu.SemaphoreType.DMA((21,)),
            pltpu.SemaphoreType.DMA((21,)),
        ],
        compiler_params=pltpu.CompilerParams(
            collective_id=0, has_side_effects=True, vmem_limit_bytes=60 * 1024 * 1024
        ),
        name="coarse",
    )(columns, live_count, aggregate, stiff_rows, stiff_iface, prolong)


def solution(mesh):
    in_specs = (
        P(("grp", "dev"), None, None, None),
        P(("grp", "dev"), None, None, None),
        P(("grp", "dev"), None),
        P(("grp", "dev")),
        P(("grp", "dev")),
        P(("grp", "dev"), None, None),
    )
    out_specs = P(("grp", "dev"), None)
    return jax.shard_map(
        on_device, mesh=mesh, in_specs=in_specs, out_specs=out_specs, check_vma=False
    )
```

time: 55.9 us -> 49.8 us (0.89)
  Pallas kernels: 52.7 us -> 46.3 us
    pallas_call x1, Pallas kernels: 52.7 us -> 46.3 us  [on_device(): pl.pallas_call(kernel, out_shape=jax.ShapeDtypeStruct((BAND // 2, 2 * HAL...]
where the time goes in v2:
time: 49.8 us; the launch traced here: 49.2 us
  Pallas kernels  46.3 us (93%)
  local copies, waits for them, and re-layouts  1.64 us (3%)
  between operations  1.3 us (3%)
    pallas_call x1, Pallas kernels, on_device(): pl.pallas_call(kernel, out_shape=jax.ShapeDtypeStruct((BAND // 2, 2 * HAL...  46.3 us
    unnamed x1, local copies, waits for them, and re-layouts  1.64 us

profile of v2, /device:TPU:1, one launch (start us, length us, event | category | flops | bytes accessed | tf_op | source)
XLA Modules:
  0.0 49.2 jit_solution(9246958338056357315)
XLA Ops:
  1.3 46.3 %coarse.1 = f32[24,2304]{1,0:T(8,128)} custom-call(s32[1,6]{1,0:T(1,128)} %cols.1, s32[1]{0:T(128)S(6)} %copy.8.live, s32[1]{0:T(128)S(6)} %copy.9.agg, bf16[1,6,384,384]{3,2,1,0:T(8,128)(2,1)} %stiff_rows.1, bf16[1,2,384,384]{3,2,1,0:T(8,128)(2,1)} %stiff_iface.1, bf16[1,384,384]{2,1,0:T(8,128)(2,1)} %prolong.1), custom_call_target="tpu_custom_call" | custom-call | tf_op jit(solution)/shard_map/coarse/pallas_call | solution.py:339
  47.6 1.6 %copy.10 = f32[24,2304]{1,0:T(8,128)} copy(f32[24,2304]{1,0:T(8,128)} %coarse.1) | data formatting | bytes 442368

commit v3 on v2

--- a/solution.py
+++ b/solution.py
@@ -35,6 +35,8 @@
     y = lax.rem(c, SIDE)
     own = 2 + k
 
+    fx, fy = 1 - k, k
+
     def at(cx, cy):
         return (g, (lax.rem(cx, SIDE) * SIDE + lax.rem(cy, SIDE)) * 2 + k)
 
@@ -46,8 +48,10 @@
     below = (jnp.maximum(g - 1, 0), d)
     has_above = g < groups - 1
     has_below = g > 0
-    along_x = [at(x + s, y) for s in (1, 2, 3)]
-    along_y = [at(x, y + s) for s in (1, 2, 3)]
+    first_at = x * fx + y * fy
+    second_at = x * fy + y * fx
+    first_line = [at(x + s * fx, y + s * fy) for s in (1, 2, 3)]
+    second_line = [at(x + s * fy, y + s * fx) for s in (1, 2, 3)]
 
     load_p = pltpu.make_async_copy(prolong.at[0], win.at[own, pl.ds(0, NB)], load_sem.at[0])
     load_b = pltpu.make_async_copy(stiff_rows.at[0], bbuf.at[pl.ds(0, SLOTS)], load_sem.at[1])
@@ -55,7 +59,7 @@
     load_p.start()
 
     barrier = pltpu.get_barrier_semaphore()
-    peers = [partner, nxt, prv, far] + along_x + along_y
+    peers = [partner, nxt, prv, far] + first_line + second_line
 
     @pl.when(has_above)
     def _():
@@ -201,8 +205,10 @@
         for coarse in range(2):
             w1 = mine_row if coarse else 1.0 - mine_row
             w2 = their_row if coarse else 1.0 - their_row
-            u = 2 * coarse + block // SIDE
-            v = lax.rem(block, SIDE)
+            to_x = 2 * coarse + block // SIDE
+            to_y = lax.rem(block, SIDE)
+            u = to_x * fx + to_y * fy
+            v = to_x * fy + to_y * fx
             dense_e[u, v, :, 0:NB] = (e1 * (w1 * (1.0 - edge_row)) + e2 * (w2 * (1.0 - edge_row2))).astype(BF)
             dense_e[u, v, :, NB:2 * NB] = (e1 * (w1 * edge_row) + e2 * (w2 * edge_row2)).astype(BF)
 
@@ -250,8 +256,8 @@
                     self.buf[self.me, v].astype(F32) + self.near[0, v].astype(F32) + self.near[1, v].astype(F32)
                 ).astype(BF)
 
-    ring_e = Ring(dense_e, far_e, near_e, sum_e, x, along_x, 2)
-    ring_m = Ring(dense_m, far_m, near_m, sum_m, y, along_y, 8)
+    ring_e = Ring(dense_e, far_e, near_e, sum_e, first_at, first_line, 2)
+    ring_m = Ring(dense_m, far_m, near_m, sum_m, first_at, first_line, 8)
     ring_e.begin()
 
     take_in(k)
@@ -273,7 +279,9 @@
         for coarse in range(2):
             w1 = mine_row if coarse else 1.0 - mine_row
             w2 = their_row if coarse else 1.0 - their_row
-            dense_m[lax.rem(block, SIDE), 2 * coarse + block // SIDE] = (m1 * w1 + m2 * w2).astype(BF)
+            to_x = 2 * coarse + block // SIDE
+            to_y = lax.rem(block, SIDE)
+            dense_m[to_x * fx + to_y * fy, to_x * fy + to_y * fx] = (m1 * w1 + m2 * w2).astype(BF)
 
     ring_m.begin()
 
@@ -284,10 +292,10 @@
         ]
 
     ring_e.end()
-    lasts = spread(sum_e, last_e, y, along_y, 13)
+    lasts = spread(sum_e, last_e, second_at, second_line, 13)
     ring_m.relay()
     ring_m.end()
-    lasts = lasts + spread(sum_m, last_m, x, along_x, 16)
+    lasts = lasts + spread(sum_m, last_m, second_at, second_line, 16)
     for copy in lasts:
         copy.wait_recv()
 
@@ -297,8 +305,8 @@
             value = value + last[number].astype(F32)
         return value.reshape(2, BAND // 2, width)
 
-    fin[:, :, 0:2 * NB] = closed(sum_e, last_e, y, 2 * NB)
-    fin[:, :, 2 * NB:HALF] = closed(sum_m, last_m, x, NB)
+    fin[:, :, 0:2 * NB] = closed(sum_e, last_e, second_at, 2 * NB)
+    fin[:, :, 2 * NB:HALF] = closed(sum_m, last_m, second_at, NB)
     swap = go(second_copy(fin.at[1 - k], got_fin, 20, partner))
 
     def place_half(side, ref):

time: 49.8 us -> 44.7 us (0.90)
  Pallas kernels: 46.3 us -> 41.5 us
    pallas_call x1, Pallas kernels: 46.3 us -> 41.5 us  [on_device(): pl.pallas_call(kernel, out_shape=jax.ShapeDtypeStruct((BAND // 2, 2 * HAL...]
where the time goes in v3:
time: 44.7 us; the launch traced here: 44.5 us
  Pallas kernels  41.5 us (93%)
  local copies, waits for them, and re-layouts  1.64 us (4%)
  between operations  1.3 us (3%)
    pallas_call x1, Pallas kernels, on_device(): pl.pallas_call(kernel, out_shape=jax.ShapeDtypeStruct((BAND // 2, 2 * HAL...  41.5 us
    unnamed x1, local copies, waits for them, and re-layouts  1.64 us

profile of v3, /device:TPU:1, one launch (start us, length us, event | category | flops | bytes accessed | tf_op | source)
XLA Modules:
  0.0 44.5 jit_solution(6977150697343506252)
XLA Ops:
  1.3 41.5 %coarse.1 = f32[24,2304]{1,0:T(8,128)} custom-call(s32[1,6]{1,0:T(1,128)} %cols.1, s32[1]{0:T(128)S(6)} %copy.8.live, s32[1]{0:T(128)S(6)} %copy.9.agg, bf16[1,6,384,384]{3,2,1,0:T(8,128)(2,1)} %stiff_rows.1, bf16[1,2,384,384]{3,2,1,0:T(8,128)(2,1)} %stiff_iface.1, bf16[1,384,384]{2,1,0:T(8,128)(2,1)} %prolong.1), custom_call_target="tpu_custom_call" | custom-call | tf_op jit(solution)/shard_map/coarse/pallas_call | solution.py:347
  42.8 1.6 %copy.10 = f32[24,2304]{1,0:T(8,128)} copy(f32[24,2304]{1,0:T(8,128)} %coarse.1) | data formatting | bytes 442368

commit v4 on v3

--- a/solution.py
+++ b/solution.py
@@ -20,7 +20,7 @@
 
 def kernel(
     cols, live, agg, stiff_rows, stiff_iface, prolong, out,
-    win, bbuf, pt, tbuf, acc, acc_e, xe, pe, xm, pm,
+    win, bbuf, pt, tbuf, acc, acc_f, tf_out, tf_in, acc_e, xe, pe, xm, pm,
     dense_e, far_e, near_e, sum_e, last_e, dense_m, far_m, near_m, sum_m, last_m, fin, got_fin,
     load_sem, send_sem, recv_sem, send2, recv2,
 ):
@@ -144,15 +144,22 @@
     def row_of(slot):
         return win[slot, NB:ROWS, :].astype(F32)[0:1, :]
 
-    def take_in(slot, fresh=False):
+    def found(slot):
         index = jnp.int32(0)
         weight = jnp.int32(0)
         for number in range(SLOTS):
             hit = (slot_of[number] == slot).astype(jnp.int32)
             index = index + hit * number
             weight = weight + hit * (number < live_now).astype(jnp.int32)
-        index = jnp.minimum(index, SLOTS - 1)
-        scale = weight.astype(F32)
+        return jnp.minimum(index, SLOTS - 1), weight.astype(F32)
+
+    index, scale = found(6)
+    tf_out[0:NB, :] = (tbuf[index].astype(F32) * scale).astype(BF)
+    tf_out[NB:ROWS, :] = win[own, NB:ROWS, :]
+    far_product = go(remote(tf_out, tf_in, send_sem.at[10], recv_sem.at[6, 0], far))
+
+    def take_in(slot, fresh=False):
+        index, scale = found(slot)
         high = row_of(slot) * scale
         low = scale - high
         value = jnp.dot(tbuf[index], win[slot, 0:NB, :], preferred_element_type=F32)
@@ -171,7 +178,6 @@
     relay_from = 4 - 3 * k
     for part in range(2):
         arrived(relay_from, part)
-        go(move(relay_from, 6, part, 10 + part, far))
         arrived(5 * k, part)
         go(move(k, k, part, 12 + part, partner))
         go(move(4 + k, 4 + k, part, 14 + part, partner))
@@ -262,26 +268,42 @@
 
     take_in(k)
     take_in(4 + k)
-    for slot in (1 - k, 5 - k, 6):
+    for slot in (1 - k, 5 - k):
         for part in range(2):
             arrived(slot, part)
         take_in(slot)
-    xm[...] = acc[1 - k].astype(BF)
+    far_product.wait_recv()
+    value = jnp.dot(tf_in[0:NB, :], win[relay_from, 0:NB, :], preferred_element_type=F32)
+    high = row_of(relay_from)
+    acc_f[0] = value * (1.0 - high)
+    acc_f[1] = value * high
+    xm[0, 0:NB, :] = acc[1 - k].astype(BF)
+    xm[0, NB:ROWS, :] = jnp.zeros((TAIL, NB), BF)
+    xm[1, 0:NB, :] = acc_f[1 - k].astype(BF)
+    xm[1, NB:ROWS, :] = tf_in[NB:ROWS, :]
     pair_m = go(second_copy(xm, pm, 1, partner))
     ring_e.relay()
     pair_m.wait_recv()
+    far_row = tf_in[NB:ROWS, :].astype(F32)[0:1, :]
+    far_row2 = pm[1, NB:ROWS, :].astype(F32)[0:1, :]
 
     @pl.loop(0, 2 * SIDE)
     def _(block):
         rows = pl.ds(pl.multiple_of(block * BAND, BAND), BAND)
         m1 = acc[k, rows, :]
-        m2 = pm[rows, :].astype(F32)
+        m2 = pm[0, rows, :].astype(F32)
+        m3 = acc_f[k, rows, :]
+        m4 = pm[1, rows, :].astype(F32)
         for coarse in range(2):
             w1 = mine_row if coarse else 1.0 - mine_row
             w2 = their_row if coarse else 1.0 - their_row
+            w3 = far_row if coarse else 1.0 - far_row
+            w4 = far_row2 if coarse else 1.0 - far_row2
             to_x = 2 * coarse + block // SIDE
             to_y = lax.rem(block, SIDE)
-            dense_m[to_x * fx + to_y * fy, to_x * fy + to_y * fx] = (m1 * w1 + m2 * w2).astype(BF)
+            dense_m[to_x * fx + to_y * fy, to_x * fy + to_y * fx] = (
+                m1 * w1 + m2 * w2 + m3 * w3 + m4 * w4
+            ).astype(BF)
 
     ring_m.begin()
 
@@ -355,11 +377,14 @@
             pltpu.VMEM((NB, NB), BF),
             pltpu.VMEM((SLOTS + 2, NB, NB), BF),
             pltpu.VMEM((2, NB, NB), F32),
+            pltpu.VMEM((2, NB, NB), F32),
+            pltpu.VMEM((ROWS, NB), BF),
+            pltpu.VMEM((ROWS, NB), BF),
             pltpu.VMEM((NB, NB), F32),
             pltpu.VMEM((ROWS, NB), BF),
             pltpu.VMEM((ROWS, NB), BF),
-            pltpu.VMEM((NB, NB), BF),
-            pltpu.VMEM((NB, NB), BF),
+            pltpu.VMEM((2, ROWS, NB), BF),
+            pltpu.VMEM((2, ROWS, NB), BF),
             *ring_buffers(2 * NB),
             *ring_buffers(NB),
             pltpu.VMEM((2, BAND // 2, HALF), F32),

time: 44.7 us -> 44.3 us (level)
  no operation moved by 1% of the time
where the time goes in v4:
time: 44.3 us; the launch traced here: 44.1 us
  Pallas kernels  41.1 us (93%)
  local copies, waits for them, and re-layouts  1.64 us (4%)
  between operations  1.3 us (3%)
    pallas_call x1, Pallas kernels, on_device(): pl.pallas_call(kernel, out_shape=jax.ShapeDtypeStruct((BAND // 2, 2 * HAL...  41.1 us
    unnamed x1, local copies, waits for them, and re-layouts  1.64 us

profile of v4, /device:TPU:1, one launch (start us, length us, event | category | flops | bytes accessed | tf_op | source)
XLA Modules:
  0.0 44.1 jit_solution(10501192563531125269)
XLA Ops:
  1.3 41.1 %coarse.1 = f32[24,2304]{1,0:T(8,128)} custom-call(s32[1,6]{1,0:T(1,128)} %cols.1, s32[1]{0:T(128)S(6)} %copy.8.live, s32[1]{0:T(128)S(6)} %copy.9.agg, bf16[1,6,384,384]{3,2,1,0:T(8,128)(2,1)} %stiff_rows.1, bf16[1,2,384,384]{3,2,1,0:T(8,128)(2,1)} %stiff_iface.1, bf16[1,384,384]{2,1,0:T(8,128)(2,1)} %prolong.1), custom_call_target="tpu_custom_call" | custom-call | tf_op jit(solution)/shard_map/coarse/pallas_call | solution.py:369
  42.4 1.6 %copy.10 = f32[24,2304]{1,0:T(8,128)} copy(f32[24,2304]{1,0:T(8,128)} %coarse.1) | data formatting | bytes 442368
